TPU v7x, 128 devices: a whole 4x4x4 slice. The times are simulated.
128 devices in a mesh: row: 16 (over y, z), col: 8 (over x, core).
Axes of the slice: x: 4, y: 4, z: 4, core: 2. Of those that a mesh axis runs over, the one named last changes fastest.
Arguments:
- noise: float32 [16384, 512], P(('row', 'col')), may hold values from -40 to 40
- data: float32 [16384, 512], P(('col', 'row')), may hold values from -6 to 6
Outputs:
- noise_target: float32 [16384, 512], P(('row', 'col'))
- data_target: float32 [16384, 512], P(('col', 'row'))
- f_potential: float32 [16384], P('row')
- g_potential: float32 [16384], P('col')
All inputs are finite; a program needn't handle non-finite values.
Results may differ from a plain program's by a relative error of at most 0.0003.
Values sent between devices are 32-bit elements; how exact they have to be, the bound alone decides.
No kernel may reach another device: no remote copies, remote signals or barrier semaphores. Data moves between devices by JAX's collectives and lax.ppermute only.
A program may use at most 64 MiB of HBM per device.

v0:
```python
import jax
import jax.numpy as jnp
from jax import lax
from jax.sharding import Mesh
from jax.sharding import PartitionSpec as P

ITERS = 2
ROW = ("row_0", "row_1")
ROW_COL = ("row_0", "row_1", "col")
COL_ROW = ("col", "row_0", "row_1")


EPSILON = 32.0


def from_everyone(shard, axis):
    size = lax.axis_size(axis)
    return lax.all_to_all(
        jnp.broadcast_to(shard[None], (size, *shard.shape)), axis, 0, 0, tiled=True
    )


def all_in_one(shard, axis):
    leaves = jax.tree.leaves(shard)
    sequence = sorted(range(len(leaves)), key=lambda k: -leaves[k].size)
    width = (1, *leaves[sequence[0]].shape)[-1]
    lines = [
        jnp.pad(leaves[k].reshape(-1), (0, -leaves[k].size % width)).reshape(-1, width)
        for k in sequence
    ]
    both, at, found = (from_everyone(jnp.concatenate(lines), axis), 0, {})
    for k, line in zip(sequence, lines):
        share = both[:, at : at + len(line)].reshape(len(both), -1)
        found[k] = share[:, : leaves[k].size].reshape(-1, *leaves[k].shape)
        at += len(line)
    numbers = iter(range(len(leaves)))
    return jax.tree.map(lambda _: found[next(numbers)], shard)


def once_a_type(shard, axis):
    leaves, found = (jax.tree.leaves(shard), {})
    for first, a in enumerate(leaves):
        if first not in found:
            alike = [k for k, b in enumerate(leaves) if b.dtype == a.dtype]
            got = (
                all_in_one([leaves[k] for k in alike], axis)
                if len(alike) > 1
                else [from_everyone(a, axis)]
            )
            for k, b in zip(alike, got):
                found[k] = b
    numbers = iter(range(len(leaves)))
    return jax.tree.map(lambda _: found[next(numbers)], shard)


def joined_by_halves(pieces, combine):
    while len(jax.tree.leaves(pieces)[0]) > 1:
        pieces = jax.vmap(combine)(
            *(jax.tree.map(lambda part: part[side::2], pieces) for side in (0, 1))
        )
    return jax.tree.map(lambda part: part[0], pieces)


def merged(shard, axis, combine):
    pieces = once_a_type(shard, axis)
    return joined_by_halves(pieces, combine)


def laid_out(parts, dim):
    parts = jnp.moveaxis(parts, 0, dim)
    shape = parts.shape
    return parts.reshape(*shape[:dim], shape[dim] * shape[dim + 1], *shape[dim + 2 :])


def collect(shard, axis, dim):
    parts = from_everyone(shard, axis)
    return laid_out(parts, dim)


def summed_rows(shard, axes, dim):
    if not axes:
        return shard
    nearer = lax.psum_scatter(shard, axes[0], scatter_dimension=dim, tiled=True)
    return summed_rows(nearer, axes[1:], dim)


def in_blocks(shard, dim, size):
    shape = shard.shape
    parts = shard.reshape(*shape[:dim], size, shape[dim] // size, *shape[dim + 1 :])
    return jnp.moveaxis(parts, dim, 0)


def summed_on_arrival(shard, axis, dim):
    size = lax.axis_size(axis)
    parts = lax.all_to_all(in_blocks(shard, dim, size), axis, 0, 0, tiled=True)
    return jnp.sum(parts, axis=0)


def combine_pair(first, second):
    peak = jnp.maximum(first[0], second[0])
    return (peak, first[1] * jnp.exp(first[0] - peak) + second[1] * jnp.exp(second[0] - peak))


def row_stats(scores):
    local_peak = jnp.max(scores, axis=1)
    local_total = jnp.sum(jnp.exp(scores - local_peak[:, None]), axis=1)
    return merged((local_peak, local_total), "col", combine_pair)


def col_stats(scores):
    local_peak = jnp.max(scores, axis=0)
    local_total = jnp.sum(jnp.exp(scores - local_peak[None, :]), axis=0)
    return merged((local_peak, local_total), ROW, combine_pair)


def shards(noise, data):
    x_full = collect(noise, "col", 0)
    y_full = lax.all_gather(data, ROW, axis=0, tiled=True)
    x_norm = jnp.sum(x_full * x_full, axis=1)
    y_norm = jnp.sum(y_full * y_full, axis=1)
    inner = jnp.dot(
        x_full, y_full.T, precision=lax.Precision.HIGHEST, preferred_element_type=jnp.float32
    )
    cost = x_norm[:, None] + y_norm[None, :] - 2.0 * inner
    g_now = jnp.zeros((cost.shape[1],), jnp.float32)
    f_now = jnp.zeros((cost.shape[0],), jnp.float32)
    col_scores = cost
    col_peak = g_now
    col_total = g_now
    for step in range(ITERS):
        row_scores = (g_now[None, :] - cost) / EPSILON
        peak, total = row_stats(row_scores)
        f_now = -EPSILON * (peak + jnp.log(total))
        col_scores = (f_now[:, None] - cost) / EPSILON
        col_peak, col_total = col_stats(col_scores)
        g_now = -EPSILON * (col_peak + jnp.log(col_total))
    col_weights = jnp.exp(col_scores - col_peak[None, :]) / col_total[None, :]
    data_part = jnp.dot(
        col_weights.T, x_full, precision=lax.Precision.HIGHEST, preferred_element_type=jnp.float32
    )
    data_target = summed_rows(data_part, ROW, 0)
    final_scores = (g_now[None, :] - cost) / EPSILON
    peak, total = row_stats(final_scores)
    weights = jnp.exp(final_scores - peak[:, None]) / total[:, None]
    noise_part = jnp.dot(
        weights, y_full, precision=lax.Precision.HIGHEST, preferred_element_type=jnp.float32
    )
    noise_target = summed_on_arrival(noise_part, "col", 0)
    return (noise_target, data_target, f_now, g_now)


def solution(mesh):
    torus = Mesh(mesh.devices.reshape(4, 4, mesh.shape["col"]), ("row_0", "row_1", "col"))
    placed = (P(ROW_COL, None), P(COL_ROW, None))
    return jax.shard_map(
        shards,
        mesh=torus,
        in_specs=placed,
        out_specs=(P(ROW_COL, None), P(COL_ROW, None), P(ROW), P("col")),
        check_vma=False,
    )
```

profile of v0, /device:TPU:0, one launch (start us, length us, event | category | flops | bytes accessed | tf_op | source)
XLA Modules:
  0.0 283.8 jit_solution(4041768908436685027)
XLA Ops:
  7.2 0.0 all-gather.2.cloned.1.call-start
  7.2 0.7 all-gather.2.cloned.1.call-update
  7.9 0.0 reduce-scatter.3.cloned.1.call-start
  7.9 1.2 broadcast_in_dim.12
  9.2 31.7 %all_to_all.35 = f32[8,128,512]{2,1,0:T(8,128)S(1)} all-to-all(f32[8,128,512]{2,1,0:T(8,128)S(1)} %broadcast_in_dim.12), channel_id=1, replica_groups=mesh['row_0'=4,'row_1'=4,'col'=8] {'col'}, dimensions={0} | all-to-all | bytes 4194304 | tf_op jit(solution)/shard_map/all_to_all | solution.py:18
  40.8 0.2 multiply_reduce_fusion.1
  41.1 23.2 %all-gather.2.cloned.1.call-done = f32[2048,512]{1,0:T(8,128)} async-done(((f32[128,512]{1,0:T(8,128)}), f32[2048,512]{1,0:T(8,128)}) %all-gather.2.cloned.1.call-update) | async-done | bytes 4194320 | tf_op jit(solution)/shard_map/all_gather | solution.py:118
  64.3 2.5 multiply_reduce_fusion
  66.8 17.0 %fusion.8 = (f32[1024]{0:T(1024)S(1)}, f32[1024,2048]{1,0:T(8,128)S(1)}) fusion(f32[1024,512]{1,0:T(8,128)S(1)} %bitcast.53, f32[2048,512]{1,0:T(8,128)} %all-gather.2.cloned.1.call-done, f32[2048]{0:T(1024)S(1)} %multiply_reduce_fusion, f32[1024]{0:T(1024)S(1)} %bitcast.97), kind=kOutput, calls=%fused_computation.19 | convolution fusion | flops 12897483776 | bytes 14696448 | tf_op jit(solution)/shard_map/dot_general | solution.py:121
  83.9 0.0 copy-start
  83.9 3.2 %copy-done = f32[1024,2048]{1,0:T(8,128)} copy-done((f32[1024,2048]{1,0:T(8,128)}, f32[1024,2048]{1,0:T(8,128)S(1)}, u32[]{:S(2)}) %copy-start) | copy-done | bytes 8388632
  87.1 2.2 exponential_reduce_fusion.4
  89.3 9.7 %all_to_all.36 = f32[8,2,1024]{2,1,0:T(2,128)S(1)} all-to-all(f32[8,2,1024]{2,1,0:T(2,128)S(1)} %broadcast_in_dim.13), channel_id=1, replica_groups=mesh['row_0'=4,'row_1'=4,'col'=8] {'col'}, dimensions={0} | all-to-all | bytes 131072 | tf_op jit(solution)/shard_map/all_to_all | solution.py:18
  99.0 0.1 fusion.36
  99.4 4.4 %fusion.9 = f32[2048]{0:T(1024)S(1)} fusion(f32[1024,2048]{1,0:T(8,128)} %copy-done, f32[1024]{0:T(1024)S(1)} %bitcast.83), kind=kLoop, calls=%fused_computation.20 | loop fusion | flops 6289408 | bytes 8400896 | tf_op jit(solution)/shard_map/reduce_max | solution.py:111
  103.8 1.3 copy-done.1
  105.1 2.3 exponential_reduce_fusion.3
  107.4 0.1 broadcast_in_dim.14
  107.5 13.6 %all_to_all.37 = f32[16,2,2048]{2,1,0:T(2,128)S(1)} all-to-all(f32[16,2,2048]{2,1,0:T(2,128)S(1)} %broadcast_in_dim.14), channel_id=1, replica_groups=mesh['row_0'=4,'row_1'=4,'col'=8] {'row_0','row_1'}, dimensions={0} | all-to-all | bytes 524288 | tf_op jit(solution)/shard_map/all_to_all | solution.py:18
  121.1 0.2 fusion.33
  121.9 0.1 add_multiply_fusion.2
  121.9 4.3 %fusion.10 = f32[1024]{0:T(1024)S(1)} fusion(f32[1024,2048]{1,0:T(8,128)} %copy-done, f32[2048]{0:T(1024)S(1)} %bitcast.75), kind=kLoop, calls=%fused_computation.21 | loop fusion | flops 6290432 | bytes 8400896 | tf_op jit(solution)/shard_map/reduce_max | solution.py:105
  126.2 4.5 %exponential_reduce_fusion.2 = f32[1024]{0:T(1024)S(1)} fusion(f32[1024,2048]{1,0:T(8,128)} %copy-done, f32[1024]{0:T(1024)S(1)} %fusion.10, f32[2048]{0:T(1024)S(1)} %bitcast.76), kind=kLoop, calls=%fused_computation.12 | loop fusion | flops 8387584 | bytes 8404992 | tf_op jit(solution)/shard_map/reduce_sum | solution.py:106
  130.8 8.0 %all_to_all.38 = f32[8,2,1024]{2,1,0:T(2,128)S(1)} all-to-all(f32[8,2,1024]{2,1,0:T(2,128)S(1)} %broadcast_in_dim.15), channel_id=1, replica_groups=mesh['row_0'=4,'row_1'=4,'col'=8] {'col'}, dimensions={0} | all-to-all | bytes 131072 | tf_op jit(solution)/shard_map/all_to_all | solution.py:18
  138.8 0.1 fusion.35
  139.2 0.0 copy-start.2
  139.2 4.3 %fusion.11 = f32[2048]{0:T(1024)S(1)} fusion(f32[1024,2048]{1,0:T(8,128)} %copy-done, f32[1024]{0:T(1024)S(1)} %bitcast.79), kind=kLoop, calls=%fused_computation.22 | loop fusion | flops 6289408 | bytes 8400896 | tf_op jit(solution)/shard_map/reduce_max | solution.py:111
  143.5 4.5 %exponential_reduce_fusion.1 = f32[2048]{0:T(1024)S(1)} fusion(f32[1024,2048]{1,0:T(8,128)} %copy-done, f32[2048]{0:T(1024)S(1)} %fusion.11, f32[1024]{0:T(1024)S(1)} %bitcast.80), kind=kLoop, calls=%fused_computation.10 | loop fusion | flops 8386560 | bytes 8409088 | tf_op jit(solution)/shard_map/reduce_sum | solution.py:112
  148.0 0.1 broadcast_in_dim.16
  148.1 11.9 %all_to_all.39 = f32[16,2,2048]{2,1,0:T(2,128)S(1)} all-to-all(f32[16,2,2048]{2,1,0:T(2,128)S(1)} %broadcast_in_dim.16), channel_id=1, replica_groups=mesh['row_0'=4,'row_1'=4,'col'=8] {'row_0','row_1'}, dimensions={0} | all-to-all | bytes 524288 | tf_op jit(solution)/shard_map/all_to_all | solution.py:18
  160.0 0.2 fusion.32
  160.8 0.1 add_multiply_fusion.1
  160.9 0.0 copy-done.2
  160.9 18.5 %fusion = f32[2048,512]{1,0:T(8,128)} fusion(f32[1024,512]{1,0:T(8,128)S(1)} %bitcast.54, f32[1024,2048]{1,0:T(8,128)} %copy-done, f32[2048]{0:T(1024)S(1)} %bitcast.87, f32[2048]{0:T(1024)S(1)} %bitcast.89, f32[1024]{0:T(1024)S(1)} %bitcast.81), kind=kOutput, calls=%fused_computation | convolution fusion | flops 12893290496 | bytes 14700544 | tf_op jit(solution)/shard_map/dot_general | solution.py:138
  179.5 0.0 reduce-scatter.3.cloned.1.call-update
  179.5 0.0 reduce-scatter.5.cloned.1.call-start
  179.5 4.3 %fusion.12 = f32[1024]{0:T(1024)S(1)} fusion(f32[1024,2048]{1,0:T(8,128)} %copy-done, f32[2048]{0:T(1024)S(1)} %bitcast.72), kind=kLoop, calls=%fused_computation.23 | loop fusion | flops 6290432 | bytes 8400896 | tf_op jit(solution)/shard_map/reduce_max | solution.py:105
  183.8 5.1 %exponential_reduce_fusion = f32[1024]{0:T(1024)S(1)} fusion(f32[1024,2048]{1,0:T(8,128)} %copy-done, f32[1024]{0:T(1024)S(1)} %fusion.12, f32[2048]{0:T(1024)S(1)} %bitcast.73), kind=kLoop, calls=%fused_computation.8 | loop fusion | flops 8387584 | bytes 8404992 | tf_op jit(solution)/shard_map/reduce_sum | solution.py:106
  189.0 8.0 %all_to_all.40 = f32[8,2,1024]{2,1,0:T(2,128)S(1)} all-to-all(f32[8,2,1024]{2,1,0:T(2,128)S(1)} %broadcast_in_dim.17), channel_id=1, replica_groups=mesh['row_0'=4,'row_1'=4,'col'=8] {'col'}, dimensions={0} | all-to-all | bytes 131072 | tf_op jit(solution)/shard_map/all_to_all | solution.py:18
  197.0 0.1 fusion.34
  197.4 25.2 %reduce-scatter.3.cloned.1.call-done = f32[512,512]{1,0:T(8,128)} async-done(((f32[2048,512]{1,0:T(8,128)}), f32[512,512]{1,0:T(8,128)}) %reduce-scatter.3.cloned.1.call-update) | async-done | bytes 1048592 | tf_op jit(solution)/shard_map/reduce_scatter | solution.py:83
  222.6 0.0 reduce-scatter.5.cloned.1.call-update
  222.6 22.3 %fusion.4 = f32[1024,512]{1,0:T(8,128)} fusion(f32[2048,512]{1,0:T(8,128)} %all-gather.2.cloned.1.call-done, f32[1024,2048]{1,0:T(8,128)} %copy-done, f32[1024]{0:T(1024)S(1)} %bitcast.98, f32[1024]{0:T(1024)S(1)} %bitcast.99, f32[2048]{0:T(1024)S(1)} %bitcast.74), kind=kOutput, calls=%fused_computation.4 | convolution fusion | flops 12893290496 | bytes 14696448 | tf_op jit(solution)/shard_map/dot_general | solution.py:145
  244.9 4.2 %all-to-all-start.6 = ((f32[8,128,512]{2,1,0:T(8,128)}), f32[8,128,512]{2,1,0:T(8,128)S(1)}, u32[]{:S(2)}, u32[]{:S(2)}) async-start(f32[8,128,512]{2,1,0:T(8,128)} %bitcast.55), calls=%async_computation.6 | async-start | bytes 4194304 | tf_op jit(solution)/shard_map/all_to_all | solution.py:95
  249.1 0.6 add_multiply_fusion
  249.8 26.6 %all-to-all-done.6 = f32[8,128,512]{2,1,0:T(8,128)S(1)} async-done(((f32[8,128,512]{2,1,0:T(8,128)}), f32[8,128,512]{2,1,0:T(8,128)S(1)}, u32[]{:S(2)}, u32[]{:S(2)}) %all-to-all-start.6) | async-done | bytes 2097184 | tf_op jit(solution)/shard_map/all_to_all | solution.py:95
  276.3 0.9 reduce_sum.79
  277.3 0.0 reduce-scatter.5.cloned.1.call-done
  (81 shorter events, 2.1 us)
Async XLA Ops:
  7.2 57.1 %all-gather.2.cloned.1.call-start = ((), (), s32[]{:S(2)}) async-start(), calls=%async_computation.9 | async-start | bytes 4456448 | tf_op jit(solution)/shard_map/all_gather | solution.py:118
  7.9 214.7 %reduce-scatter.3.cloned.1.call-start = ((), (), s32[]{:S(2)}) async-start(), calls=%async_computation.10 | async-start | bytes 5242880 | tf_op jit(solution)/shard_map/reduce_scatter | solution.py:83
  83.9 3.2 %copy-start = (f32[1024,2048]{1,0:T(8,128)}, f32[1024,2048]{1,0:T(8,128)S(1)}, u32[]{:S(2)}) copy-start(f32[1024,2048]{1,0:T(8,128)S(1)} %get-tuple-element.44) | copy-start | bytes 25165828
  99.3 5.8 %copy-start.1 = (f32[1024,2048]{1,0:T(8,128)S(1)}, f32[1024,2048]{1,0:T(8,128)}, u32[]{:S(2)}) copy-start(f32[1024,2048]{1,0:T(8,128)} %copy-done) | copy-start | bytes 25165828
  139.2 21.7 %copy-start.2 = (f32[1,1024]{1,0:T(1,128)}, f32[1,1024]{1,0:T(1,128)S(1)}, u32[]{:S(2)}) copy-start(f32[1,1024]{1,0:T(1,128)S(1)} %add_multiply_fusion.3) | copy-start | bytes 12292
  179.5 97.8 %reduce-scatter.5.cloned.1.call-start = ((), (), s32[]{:S(2)}) async-start(), calls=%async_computation.11 | async-start | bytes 1310720 | tf_op jit(solution)/shard_map/reduce_scatter | solution.py:83
  244.9 31.4 %all-to-all-start.6 = ((f32[8,128,512]{2,1,0:T(8,128)}), f32[8,128,512]{2,1,0:T(8,128)S(1)}, u32[]{:S(2)}, u32[]{:S(2)}) async-start(f32[8,128,512]{2,1,0:T(8,128)} %bitcast.55), calls=%async_computation.6 | async-start | bytes 4194304 | tf_op jit(solution)/shard_map/all_to_all | solution.py:95
Sparse Core Ops, SparseCore 0:
  10.1 54.1 all-gather.1
  179.6 42.9 reduce-scatter.2
  225.7 23.3 reduce-scatter.4
where the time goes:
time: 285 us; the launch traced here: 284 us
  blocking collectives  82.9 us (29%)
  waiting for transfers between devices  75.8 us (27%)
  matrix products  57.9 us (20%)
  other arithmetic  40.7 us (14%)
  between operations  14.1 us (5%)
  local copies, waits for them, and re-layouts  8.01 us (3%)
  starting transfers between devices  4.35 us (2%)
    all_to_all x6, blocking collectives, from_everyone(): lax.all_to_all(jnp.broadcast_to(shard[None], (size, *shard.shape)), axis,...  82.9 us
    all_to_all x1, waiting for transfers between devices, summed_on_arrival(): parts = lax.all_to_all(in_blocks(shard, dim, size), axis, 0, 0, tiled=True)  26.6 us
    reduce_scatter x2, waiting for transfers between devices, summed_rows(): nearer = lax.psum_scatter(shard, axes[0], scatter_dimension=dim, tiled=True)  25.2 us
    all_gather x1, waiting for transfers between devices, shards(): y_full = lax.all_gather(data, ROW, axis=0, tiled=True)  23.2 us
    dot_general x1, matrix products, shards(): jnp.dot(weights, y_full, precision=lax.Precision.HIGHEST, preferred_eleme...  22.3 us
    dot_general x1, matrix products, shards(): jnp.dot(col_weights.T, x_full, precision=lax.Precision.HIGHEST, preferred...  18.5 us
    dot_general x1, matrix products, shards(): jnp.dot(x_full, y_full.T, precision=lax.Precision.HIGHEST, preferred_elem...  17 us
    reduce_sum x3, other arithmetic, row_stats(): local_total = jnp.sum(jnp.exp(scores - local_peak[:, None]), axis=1)  11.8 us
  transfers between devices with their start and end apart: 4, of which 3 were waited for; matrix products, arithmetic and copies ran while one was open for 12% of the time, Pallas kernels for 0%

commit v1 on v0

v1 whole, which is shorter than its diff:
```python
import jax
import jax.numpy as jnp
from jax import lax
from jax.experimental import pallas as pl
from jax.experimental.pallas import tpu as pltpu
from jax.sharding import Mesh
from jax.sharding import PartitionSpec as P

ROW = ("row_0", "row_1")
ROW_COL = ("row_0", "row_1", "col")
COL_ROW = ("col", "row_0", "row_1")

EPSILON = 32.0
LOG2E = 1.4426950408889634
LN2 = 0.6931471805599453
SCALE = LOG2E / EPSILON
BLOCK = 256
VMEM_LIMIT = 48 * 1024 * 1024


def from_everyone(shard, axis):
    size = lax.axis_size(axis)
    return lax.all_to_all(
        jnp.broadcast_to(shard[None], (size, *shard.shape)), axis, 0, 0, tiled=True
    )


def split(v):
    high = v.astype(jnp.bfloat16)
    return high, (v - high.astype(jnp.float32)).astype(jnp.bfloat16)


def dot(a, b, dims):
    return lax.dot_general(a, b, (dims, ((), ())), preferred_element_type=jnp.float32)


def as_column(row):
    return jnp.broadcast_to(row, (128, row.shape[1])).T


def as_row(column):
    return column.T[0:1, :]


def call(kernel, grid, in_specs, out_specs, out_shape, scratch=(), cost=None):
    return pl.pallas_call(
        kernel,
        grid=grid,
        in_specs=in_specs,
        out_specs=out_specs,
        out_shape=out_shape,
        scratch_shapes=scratch,
        cost_estimate=cost,
        compiler_params=pltpu.CompilerParams(
            dimension_semantics=("arbitrary",), vmem_limit_bytes=VMEM_LIMIT
        ),
    )


def whole(shape):
    return pl.BlockSpec(shape, lambda j: (0,) * len(shape))


def f32(*shape):
    return jax.ShapeDtypeStruct(shape, jnp.float32)


def scores_kernel(x_ref, y_ref, s_ref, lse_ref, xh, xl, peak, scores, bias):
    j = pl.program_id(0)
    last = pl.num_programs(0) - 1

    @pl.when(j == 0)
    def _():
        xh[...], xl[...] = split(x_ref[...] * (2.0 * SCALE))
        peak[...] = jnp.full_like(peak, -jnp.inf)

    y = y_ref[...]
    yh, yl = split(y)
    lanes = ((1,), (1,))
    s = dot(xh[...], yh, lanes) + (dot(xh[...], yl, lanes) + dot(xl[...], yh, lanes))
    norm = as_row(jnp.broadcast_to(jnp.sum(y * y, axis=1, keepdims=True), (BLOCK, 128)))
    shift = -SCALE * norm
    s_ref[...] = s
    scores[j] = s
    bias[j] = jnp.broadcast_to(shift, (8, BLOCK))
    t = s + shift
    peak[...] = jnp.maximum(peak[...], jnp.maximum(t[:, :128], t[:, 128:]))

    @pl.when(j == last)
    def _():
        top = jnp.max(peak[...], axis=1, keepdims=True)

        def add(k, total):
            e = jnp.exp2(scores[k] + (bias[k][0:1, :] - top))
            return total + (e[:, :128] + e[:, 128:])

        total = lax.fori_loop(0, pl.num_programs(0), add, jnp.zeros_like(peak))
        total = jnp.sum(total, axis=1, keepdims=True)
        lse = top + jnp.log2(total)
        lse_ref[...] = as_row(jnp.broadcast_to(lse, peak.shape))


def scores_of(x, y):
    n, w = x.shape
    m = y.shape[0]
    steps = m // BLOCK
    return call(
        scores_kernel,
        (steps,),
        [whole((n, w)), pl.BlockSpec((BLOCK, w), lambda j: (j, 0))],
        [pl.BlockSpec((n, BLOCK), lambda j: (0, j)), whole((1, n))],
        (f32(n, m), f32(1, n)),
        (
            pltpu.VMEM((n, w), jnp.bfloat16),
            pltpu.VMEM((n, w), jnp.bfloat16),
            pltpu.VMEM((n, 128), jnp.float32),
            pltpu.VMEM((steps, n, BLOCK), jnp.float32),
            pltpu.VMEM((steps, 8, BLOCK), jnp.float32),
        ),
        pl.CostEstimate(flops=6 * n * m * w, bytes_accessed=4 * n * m, transcendentals=n * m),
    )(x, y)


def negative_lse(parts):
    top = jnp.max(parts, axis=0, keepdims=True)
    return -(top + jnp.log2(jnp.sum(jnp.exp2(parts - top), axis=0, keepdims=True)))


def columns_kernel(s_ref, parts_ref, qh_ref, ql_ref, top_ref, lse_ref, a_ref, a_col):
    @pl.when(pl.program_id(0) == 0)
    def _():
        a = negative_lse(parts_ref[...])
        a_ref[...] = a
        a_col[...] = as_column(a)

    a = a_col[...]
    s = s_ref[...] + jnp.concatenate([a] * (BLOCK // 128), axis=1)
    top = jnp.max(s, axis=0, keepdims=True)
    q = jnp.exp2(s - top)
    qh_ref[...], ql_ref[...] = split(q)
    top_ref[...] = top
    lse_ref[...] = top + jnp.log2(jnp.sum(q, axis=0, keepdims=True))


def columns_of(s, parts):
    n, m = s.shape
    block = pl.BlockSpec((n, BLOCK), lambda j: (0, j))
    line = pl.BlockSpec((1, BLOCK), lambda j: (0, j))
    return call(
        columns_kernel,
        (m // BLOCK,),
        [block, whole(parts.shape)],
        [block, block, line, line, whole((1, n))],
        (
            jax.ShapeDtypeStruct((n, m), jnp.bfloat16),
            jax.ShapeDtypeStruct((n, m), jnp.bfloat16),
            f32(1, m),
            f32(1, m),
            f32(1, n),
        ),
        (pltpu.VMEM((n, 128), jnp.float32),),
        pl.CostEstimate(flops=4 * n * m, bytes_accessed=8 * n * m, transcendentals=n * m),
    )(s, parts)


def rows_kernel(qh_ref, ql_ref, top_ref, parts_ref, sum_ref, t_ref, b_ref, total):
    j = pl.program_id(0)

    @pl.when(j == 0)
    def _():
        total[...] = jnp.zeros_like(total)

    b = negative_lse(parts_ref[...])
    t = jnp.exp2(top_ref[...] + b)
    b_ref[...] = b
    t_ref[...] = t
    p = (qh_ref[...].astype(jnp.float32) + ql_ref[...].astype(jnp.float32)) * t
    total[...] += p[:, :128] + p[:, 128:]

    @pl.when(j == pl.num_programs(0) - 1)
    def _():
        rows = jnp.sum(total[...], axis=1, keepdims=True)
        sum_ref[...] = as_row(jnp.broadcast_to(rows, total.shape))


def row_sums(qh, ql, top, parts):
    n, m = qh.shape
    block = pl.BlockSpec((n, BLOCK), lambda j: (0, j))
    line = pl.BlockSpec((1, BLOCK), lambda j: (0, j))
    return call(
        rows_kernel,
        (m // BLOCK,),
        [block, block, line, pl.BlockSpec((parts.shape[0], BLOCK), lambda j: (0, j))],
        [whole((1, n)), line, line],
        (f32(1, n), f32(1, m), f32(1, m)),
        (pltpu.VMEM((n, 128), jnp.float32),),
        pl.CostEstimate(flops=4 * n * m, bytes_accessed=4 * n * m, transcendentals=0),
    )(qh, ql, top, parts)


def column_sums_kernel(qh_ref, ql_ref, parts_ref, t_ref, sum_ref, r_ref, inv):
    @pl.when(pl.program_id(0) == 0)
    def _():
        r = jnp.sum(parts_ref[...], axis=0, keepdims=True)
        r_ref[...] = r
        inv[...] = as_column(1.0 / r)

    scale = jnp.concatenate([inv[...]] * (BLOCK // 128), axis=1)
    q = (qh_ref[...].astype(jnp.float32) + ql_ref[...].astype(jnp.float32)) * scale
    sum_ref[...] = jnp.sum(q, axis=0, keepdims=True) * t_ref[...]


def column_sums(qh, ql, parts, t):
    n, m = qh.shape
    block = pl.BlockSpec((n, BLOCK), lambda j: (0, j))
    line = pl.BlockSpec((1, BLOCK), lambda j: (0, j))
    return call(
        column_sums_kernel,
        (m // BLOCK,),
        [block, block, whole(parts.shape), line],
        [line, whole((1, n))],
        (f32(1, m), f32(1, n)),
        (pltpu.VMEM((n, 128), jnp.float32),),
        pl.CostEstimate(flops=4 * n * m, bytes_accessed=4 * n * m, transcendentals=0),
    )(qh, ql, parts, t)


def data_kernel(qh_ref, ql_ref, t_ref, r_ref, x_ref, out_ref, xt):
    w = x_ref.shape[1]

    @pl.when(pl.program_id(0) == 0)
    def _():
        inv = as_column(1.0 / r_ref[...])
        scaled = x_ref[...] * jnp.concatenate([inv] * (w // 128), axis=1)
        high, low = split(scaled.T)
        xt[:w, :] = high
        xt[w:, :] = low

    inner = ((1,), (0,))
    both = dot(xt[...], qh_ref[...], inner)
    part = both[:w] + (both[w:] + dot(xt[:w, :], ql_ref[...], inner))
    out_ref[...] = (part * t_ref[...]).T


def data_part_of(qh, ql, t, r, x):
    n, m = qh.shape
    w = x.shape[1]
    block = pl.BlockSpec((n, BLOCK), lambda j: (0, j))
    return call(
        data_kernel,
        (m // BLOCK,),
        [
            block,
            block,
            pl.BlockSpec((1, BLOCK), lambda j: (0, j)),
            whole((1, n)),
            whole((n, w)),
        ],
        pl.BlockSpec((BLOCK, w), lambda j: (j, 0)),
        f32(m, w),
        (pltpu.VMEM((2 * w, n), jnp.bfloat16),),
        pl.CostEstimate(flops=6 * n * m * w, bytes_accessed=4 * n * m, transcendentals=0),
    )(qh, ql, t, r, x)


def noise_kernel(qh_ref, ql_ref, parts_ref, t_ref, y_ref, out_ref, c_ref, acc, total):
    j = pl.program_id(0)
    w = y_ref.shape[1]

    @pl.when(j == 0)
    def _():
        acc[...] = jnp.zeros_like(acc)
        total[...] = jnp.zeros_like(total)

    c = jnp.sum(parts_ref[...], axis=0, keepdims=True)
    c_ref[...] = c
    scale = t_ref[...] / c
    yh, yl = split(y_ref[...] * jnp.concatenate([as_column(scale)] * (w // 128), axis=1))
    qh, ql = qh_ref[...], ql_ref[...]
    inner = ((1,), (0,))
    acc[...] += dot(qh, yh, inner) + (dot(qh, yl, inner) + dot(ql, yh, inner))
    p = (qh.astype(jnp.float32) + ql.astype(jnp.float32)) * scale
    total[...] += p[:, :128] + p[:, 128:]

    @pl.when(j == pl.num_programs(0) - 1)
    def _():
        rows = jnp.sum(total[...], axis=1, keepdims=True)
        line = as_row(jnp.broadcast_to(rows, total.shape))
        for k in range(out_ref.shape[0]):
            at = slice(k * 128, (k + 1) * 128)
            out_ref[k, :128, :] = acc[at, :]
            out_ref[k, 128:, :] = jnp.broadcast_to(
                jnp.concatenate([line[:, at]] * (w // 128), axis=1), (8, w)
            )


def noise_part_of(qh, ql, parts, t, y):
    n, m = qh.shape
    w = y.shape[1]
    block = pl.BlockSpec((n, BLOCK), lambda j: (0, j))
    line = pl.BlockSpec((1, BLOCK), lambda j: (0, j))
    return call(
        noise_kernel,
        (m // BLOCK,),
        [
            block,
            block,
            pl.BlockSpec((parts.shape[0], BLOCK), lambda j: (0, j)),
            line,
            pl.BlockSpec((BLOCK, w), lambda j: (j, 0)),
        ],
        [whole((n // 128, 136, w)), line],
        (f32(n // 128, 136, w), f32(1, m)),
        (pltpu.VMEM((n, w), jnp.float32), pltpu.VMEM((n, 128), jnp.float32)),
        pl.CostEstimate(flops=6 * n * m * w, bytes_accessed=4 * n * m, transcendentals=0),
    )(qh, ql, parts, t, y)


def gathered(line, axis):
    n = line.shape[1]
    return from_everyone(line.reshape(n // 128, 128), axis).reshape(-1, n)


def shards(noise, data):
    x = from_everyone(noise, "col").reshape(-1, noise.shape[1])
    y = lax.all_gather(data, ROW, axis=0, tiled=True)
    s, row_lse = scores_of(x, y)
    qh, ql, top, col_lse, a = columns_of(s, gathered(row_lse, "col"))
    row_part, t, b = row_sums(qh, ql, top, gathered(col_lse, ROW))
    col_part, r = column_sums(qh, ql, gathered(row_part, "col"), t)
    data_part = data_part_of(qh, ql, t, r, x)
    for axis in ROW:
        data_part = lax.psum_scatter(data_part, axis, scatter_dimension=0, tiled=True)
    noise_part, c = noise_part_of(qh, ql, gathered(col_part, ROW), t, y)
    noise_sum = jnp.sum(lax.all_to_all(noise_part, "col", 0, 0, tiled=True), axis=0)
    noise_target = noise_sum[:128] / noise_sum[128, :128][:, None]
    x_norm = jnp.sum(x * x, axis=1)
    y_norm = jnp.sum(y * y, axis=1)
    me = lax.axis_index(ROW)
    mine = lax.dynamic_slice(c, (0, me * 128), (1, 128))
    data_target = data_part / mine.reshape(128, 1)
    f = x_norm + (LN2 * EPSILON) * (a - jnp.log2(r)).reshape(-1)
    g = y_norm + (LN2 * EPSILON) * (b - jnp.log2(c)).reshape(-1)
    return noise_target, data_target, f, g


def solution(mesh):
    torus = Mesh(mesh.devices.reshape(4, 4, mesh.shape["col"]), ("row_0", "row_1", "col"))
    placed = (P(ROW_COL, None), P(COL_ROW, None))
    return jax.shard_map(
        shards,
        mesh=torus,
        in_specs=placed,
        out_specs=(P(ROW_COL, None), P(COL_ROW, None), P(ROW), P("col")),
        check_vma=False,
    )
```

time: 285 us -> 223 us (0.78)
  Pallas kernels: 0 us -> 61.1 us
  matrix products: 57.9 us -> 0 us
  other arithmetic: 40.7 us -> 8.42 us
  waiting for transfers between devices: 75.8 us -> 56.6 us
  blocking collectives: 82.9 us -> 74.1 us
  local copies, waits for them, and re-layouts: 8.01 us -> 2.69 us
    pallas_call x0 -> x6, Pallas kernels: none -> 61.1 us  [the longest x1 15.5 us: scores_of(): call(scores_kernel, (steps,), [whole((n, w)), pl.BlockSpec((BLOCK, w), la...]
    dot_general x3 -> x0, matrix products: 57.9 us -> none  [the longest x1 22.3 us: shards(): jnp.dot(weights, y_full, precision=lax.Precision.HIGHEST, preferred_eleme...]
    reduce_sum x8 -> x3, other arithmetic: 22.2 us -> 4.65 us  [the longest x1 2.54 us: shards(): y_norm = jnp.sum(y * y, axis=1)]
    reduce_max x4 -> x0, other arithmetic: 17.3 us -> none  [the longest x2 8.69 us: col_stats(): local_peak = jnp.max(scores, axis=0)]
    all_to_all x1, waiting for transfers between devices: 26.6 us -> 10.7 us  [shards(): lax.all_to_all(noise_part, 'col', 0, 0, tiled=True)]
    all_to_all x6 -> x5, blocking collectives: 82.9 us -> 74.1 us  [from_everyone(): lax.all_to_all(jnp.broadcast_to(shard[None], (size, *shard.shape)), axis,...]
    reduce_scatter x2, waiting for transfers between devices: 25.2 us -> 21.8 us  [shards(): lax.psum_scatter(data_part, axis, scatter_dimension=0, tiled=True)]
    unnamed x14 -> x8, local copies, waits for them, and re-layouts: 4.69 us -> 1.46 us
  transfers between devices with their start and end apart: 4 -> 4, of which waited for: 3 -> 4; matrix products, arithmetic and copies ran while one was open for 12% -> 4% of each run, Pallas kernels for 0% -> 5%
where the time goes in v1:
time: 223 us; the launch traced here: 221 us
  blocking collectives  74.1 us (33%)
  Pallas kernels  61.1 us (27%)
  waiting for transfers between devices  56.6 us (25%)
  between operations  13.9 us (6%)
  other arithmetic  8.42 us (4%)
  starting transfers between devices  4.47 us (2%)
  local copies, waits for them, and re-layouts  2.69 us (1%)
    all_to_all x5, blocking collectives, from_everyone(): lax.all_to_all(jnp.broadcast_to(shard[None], (size, *shard.shape)), axis,...  74.1 us
    all_gather x1, waiting for transfers between devices, shards(): y = lax.all_gather(data, ROW, axis=0, tiled=True)  23.5 us
    reduce_scatter x2, waiting for transfers between devices, shards(): lax.psum_scatter(data_part, axis, scatter_dimension=0, tiled=True)  21.8 us
    pallas_call x1, Pallas kernels, scores_of(): call(scores_kernel, (steps,), [whole((n, w)), pl.BlockSpec((BLOCK, w), la...  15.5 us
    pallas_call x1, Pallas kernels, data_part_of(): call(data_kernel, (m // BLOCK,), [block, block, pl.BlockSpec((1, BLOCK),...  12.5 us
    pallas_call x1, Pallas kernels, noise_part_of(): call(noise_kernel, (m // BLOCK,), [block, block, pl.BlockSpec((parts.shap...  11.9 us
    all_to_all x1, waiting for transfers between devices, shards(): lax.all_to_all(noise_part, 'col', 0, 0, tiled=True)  10.7 us
    pallas_call x1, Pallas kernels, columns_of(): call(columns_kernel, (m // BLOCK,), [block, whole(parts.shape)], [block,...  9.34 us
  transfers between devices with their start and end apart: 4, of which 4 were waited for; matrix products, arithmetic and copies ran while one was open for 4% of the time, Pallas kernels for 5%

profile of v1, /device:TPU:0, one launch (start us, length us, event | category | flops | bytes accessed | tf_op | source)
XLA Modules:
  0.0 221.3 jit_solution(6760438911168544492)
XLA Ops:
  7.2 0.0 all-gather.2.cloned.1.call-start
  7.2 0.7 all-gather.2.cloned.1.call-update
  7.9 0.0 reduce-scatter.3.cloned.1.call-start
  7.9 1.2 broadcast_in_dim.34
  9.2 31.7 %all_to_all.30 = f32[8,128,512]{2,1,0:T(8,128)S(1)} all-to-all(f32[8,128,512]{2,1,0:T(8,128)S(1)} %broadcast_in_dim.34), channel_id=1, replica_groups=mesh['row_0'=4,'row_1'=4,'col'=8] {'col'}, dimensions={0} | all-to-all | bytes 4194304 | tf_op jit(solution)/shard_map/all_to_all | solution.py:23
  40.8 23.5 %all-gather.2.cloned.1.call-done.y_ref = f32[2048,512]{1,0:T(8,128)} async-done(((f32[128,512]{1,0:T(8,128)}), f32[2048,512]{1,0:T(8,128)}) %all-gather.2.cloned.1.call-update) | async-done | bytes 4194320 | tf_op jit(solution)/shard_map/all_gather | solution.py:326
  64.3 15.5 %shard_map.57 = (f32[1024,2048]{1,0:T(8,128)}, f32[1,1024]{1,0:T(1,128)S(1)}) custom-call(f32[1024,512]{1,0:T(8,128)S(1)} %bitcast.29, f32[2048,512]{1,0:T(8,128)} %all-gather.2.cloned.1.call-done.y_ref), custom_call_target="tpu_custom_call" | custom-call | flops 6442450944 | bytes 8388608 | tf_op jit(solution)/shard_map/pallas_call | solution.py:107
  79.8 9.5 %all_to_all.31 = f32[8,8,128]{2,1,0:T(8,128)S(1)} all-to-all(f32[8,8,128]{2,1,0:T(8,128)S(1)} %broadcast_in_dim.36), channel_id=1, replica_groups=mesh['row_0'=4,'row_1'=4,'col'=8] {'col'}, dimensions={0} | all-to-all | bytes 65536 | tf_op jit(solution)/shard_map/all_to_all | solution.py:23
  89.3 9.3 %shard_map.58 = (bf16[1024,2048]{1,0:T(8,128)(2,1)S(1)}, bf16[1024,2048]{1,0:T(8,128)(2,1)}, f32[1,2048]{1,0:T(1,128)S(1)}, f32[1,2048]{1,0:T(1,128)S(1)}, f32[1,1024]{1,0:T(1,128)S(1)}) custom-call(f32[1024,2048]{1,0:T(8,128)} %get-tuple-element.18.s_ref, f32[8,1024]{1,0:T(8,128)S(1)} %bitcast.32), custom_call_target="tpu_custom_call" | custom-call | flops 8388608 | bytes 16777216 | tf_op jit(solution)/shard_map/pallas_call | solution.py:149
  98.6 0.0 copy-start
  98.6 12.9 %all_to_all.32 = f32[16,16,128]{2,1,0:T(8,128)S(1)} all-to-all(f32[16,16,128]{2,1,0:T(8,128)S(1)} %broadcast_in_dim.38), channel_id=1, replica_groups=mesh['row_0'=4,'row_1'=4,'col'=8] {'row_0','row_1'}, dimensions={0} | all-to-all | bytes 262144 | tf_op jit(solution)/shard_map/all_to_all | solution.py:23
  111.6 6.0 %shard_map.59 = (f32[1,1024]{1,0:T(1,128)S(1)}, f32[1,2048]{1,0:T(1,128)S(1)}, f32[1,2048]{1,0:T(1,128)S(1)}) custom-call(bf16[1024,2048]{1,0:T(8,128)(2,1)S(1)} %get-tuple-element.20.qh_ref, bf16[1024,2048]{1,0:T(8,128)(2,1)} %get-tuple-element.21.ql_ref, f32[1,2048]{1,0:T(1,128)S(1)} %get-tuple-element.22.top_ref, f32[16,2048]{1,0:T(8,128)S(1)} %bitcast.31), custom_call_target="tpu_custom_call" | custom-call | flops 8388608 | bytes 8388608 | tf_op jit(solution)/shard_map/pallas_call | solution.py:190
  117.6 7.8 %all_to_all.33 = f32[8,8,128]{2,1,0:T(8,128)S(1)} all-to-all(f32[8,8,128]{2,1,0:T(8,128)S(1)} %broadcast_in_dim.40), channel_id=1, replica_groups=mesh['row_0'=4,'row_1'=4,'col'=8] {'col'}, dimensions={0} | all-to-all | bytes 65536 | tf_op jit(solution)/shard_map/all_to_all | solution.py:23
  125.4 0.0 copy-done
  125.4 6.0 %shard_map.60 = (f32[1,2048]{1,0:T(1,128)S(1)}, f32[1,1024]{1,0:T(1,128)S(1)}) custom-call(bf16[1024,2048]{1,0:T(8,128)(2,1)S(1)} %get-tuple-element.20.qh_ref, bf16[1024,2048]{1,0:T(8,128)(2,1)} %get-tuple-element.21.ql_ref, f32[8,1024]{1,0:T(8,128)S(1)} %bitcast.33, f32[1,2048]{1,0:T(1,128)S(1)} %get-tuple-element.25.t_ref), custom_call_target="tpu_custom_call" | custom-call | flops 8388608 | bytes 8388608 | tf_op jit(solution)/shard_map/pallas_call | solution.py:217
  131.4 12.5 %shard_map.62 = f32[2048,512]{1,0:T(8,128)} custom-call(bf16[1024,2048]{1,0:T(8,128)(2,1)} %copy-done, bf16[1024,2048]{1,0:T(8,128)(2,1)} %get-tuple-element.21.ql_ref, f32[1,2048]{1,0:T(1,128)S(1)} %get-tuple-element.25.t_ref, f32[1,1024]{1,0:T(1,128)S(1)} %get-tuple-element.28.r_ref, f32[1024,512]{1,0:T(8,128)S(1)} %bitcast.30), custom_call_target="tpu_custom_call" | custom-call | flops 6442450944 | bytes 8388608 | tf_op jit(solution)/shard_map/pallas_call | solution.py:249
  143.9 0.0 reduce-scatter.3.cloned.1.call-update
  144.0 12.2 %all_to_all.34 = f32[16,16,128]{2,1,0:T(8,128)S(1)} all-to-all(f32[16,16,128]{2,1,0:T(8,128)S(1)} %broadcast_in_dim.42), channel_id=1, replica_groups=mesh['row_0'=4,'row_1'=4,'col'=8] {'row_0','row_1'}, dimensions={0} | all-to-all | bytes 262144 | tf_op jit(solution)/shard_map/all_to_all | solution.py:23
  156.2 11.9 %shard_map.61 = (f32[8,136,512]{2,1,0:T(8,128)S(1)}, f32[1,2048]{1,0:T(1,128)S(1)}) custom-call(bf16[1024,2048]{1,0:T(8,128)(2,1)} %copy-done, bf16[1024,2048]{1,0:T(8,128)(2,1)} %get-tuple-element.21.ql_ref, f32[16,2048]{1,0:T(8,128)S(1)} %bitcast.34, f32[1,2048]{1,0:T(1,128)S(1)} %get-tuple-element.25.t_ref, f32[2048,512]{1,0:T(8,128)} %all-gather.2.cloned.1.call-done.y_ref), custom_call_target="tpu_custom_call" | custom-call | flops 6442450944 | bytes 8388608 | tf_op jit(solution)/shard_map/pallas_call | solution.py:302
  168.1 0.0 copy-start.1
  168.1 1.4 copy-done.1
  169.4 4.4 %all-to-all-start.5 = ((f32[8,136,512]{2,1,0:T(8,128)}), f32[8,136,512]{2,1,0:T(8,128)}, u32[]{:S(2)}, u32[]{:S(2)}) async-start(f32[8,136,512]{2,1,0:T(8,128)} %copy-done.1), calls=%async_computation.5 | async-start | bytes 4456448 | tf_op jit(solution)/shard_map/all_to_all | solution.py:335
  173.8 0.0 reduce-scatter.5.cloned.1.call-start
  173.8 13.8 %reduce-scatter.3.cloned.1.call-done = f32[512,512]{1,0:T(8,128)} async-done(((f32[2048,512]{1,0:T(8,128)}), f32[512,512]{1,0:T(8,128)}) %reduce-scatter.3.cloned.1.call-update) | async-done | bytes 1048592 | tf_op jit(solution)/shard_map/reduce_scatter | solution.py:333
  187.7 0.0 reduce-scatter.5.cloned.1.call-update
  187.7 0.2 multiply_reduce_fusion.1
  187.9 2.5 %multiply_reduce_fusion = f32[2048]{0:T(1024)S(1)} fusion(f32[2048,512]{1,0:T(8,128)} %all-gather.2.cloned.1.call-done.y_ref), kind=kLoop, calls=%fused_computation | loop fusion | flops 2095104 | bytes 4202496 | tf_op jit(solution)/shard_map/reduce_sum | solution.py:338
  190.5 0.6 bitcast_add_fusion
  191.1 0.6 add.19
  191.7 10.7 %all-to-all-done.5 = f32[8,136,512]{2,1,0:T(8,128)} async-done(((f32[8,136,512]{2,1,0:T(8,128)}), f32[8,136,512]{2,1,0:T(8,128)}, u32[]{:S(2)}, u32[]{:S(2)}) %all-to-all-start.5) | async-done | bytes 2228256 | tf_op jit(solution)/shard_map/all_to_all | solution.py:335
  202.4 1.9 reduce_sum.29
  204.3 0.8 slice_divide_fusion
  205.1 7.9 %reduce-scatter.5.cloned.1.call-done = f32[128,512]{1,0:T(8,128)} async-done(((f32[512,512]{1,0:T(8,128)}), f32[128,512]{1,0:T(8,128)}) %reduce-scatter.5.cloned.1.call-update) | async-done | bytes 262160 | tf_op jit(solution)/shard_map/reduce_scatter | solution.py:333
  213.0 1.7 broadcast_divide_fusion
  (12 shorter events, 0.2 us)
Async XLA Ops:
  7.2 57.1 %all-gather.2.cloned.1.call-start = ((), (), s32[]{:S(2)}) async-start(), calls=%async_computation.8 | async-start | bytes 4456448 | tf_op jit(solution)/shard_map/all_gather | solution.py:326
  7.9 179.8 %reduce-scatter.3.cloned.1.call-start = ((), (), s32[]{:S(2)}) async-start(), calls=%async_computation.9 | async-start | bytes 5242880 | tf_op jit(solution)/shard_map/reduce_scatter | solution.py:333
  98.6 26.8 %copy-start = (bf16[1024,2048]{1,0:T(8,128)(2,1)}, bf16[1024,2048]{1,0:T(8,128)(2,1)S(1)}, u32[]{:S(2)}) copy-start(bf16[1024,2048]{1,0:T(8,128)(2,1)S(1)} %get-tuple-element.20.qh_ref) | copy-start | bytes 12582916
  168.1 1.4 copy-start.1
  169.4 33.0 %all-to-all-start.5 = ((f32[8,136,512]{2,1,0:T(8,128)}), f32[8,136,512]{2,1,0:T(8,128)}, u32[]{:S(2)}, u32[]{:S(2)}) async-start(f32[8,136,512]{2,1,0:T(8,128)} %copy-done.1), calls=%async_computation.5 | async-start | bytes 4456448 | tf_op jit(solution)/shard_map/all_to_all | solution.py:335
  173.8 39.2 %reduce-scatter.5.cloned.1.call-start = ((), (), s32[]{:S(2)}) async-start(), calls=%async_computation.10 | async-start | bytes 1310720 | tf_op jit(solution)/shard_map/reduce_scatter | solution.py:333
Sparse Core Ops, SparseCore 0:
  10.1 54.1 all-gather.1
  144.1 43.5 reduce-scatter.2
  190.2 22.7 reduce-scatter.4
